TPU v7x, 32 devices: a whole 2x2x4 slice. The times are simulated.
32 devices in a mesh: groups: 2 (over x), gx: 4 (over y, core), gy: 4 (over z).
Axes of the slice: x: 2, y: 2, z: 4, core: 2. Of those that a mesh axis runs over, the one named last changes fastest.
Arguments:
- coarse_field: bfloat16 [64, 8, 16, 64], P('groups', 'gx', 'gy'), parts along dimension 0, may hold values from -6 to 6
- skip_field: bfloat16 [64, 16, 32, 128], P('groups', 'gx', 'gy'), parts along dimension 0, may hold values from -6 to 6
- cotangent: bfloat16 [64, 16, 32, 128], P('groups', 'gx', 'gy'), parts along dimension 0, may hold values from -6 to 6
- up_kernel: bfloat16 [32, 32, 3, 3, 3], replicated, may hold values from -0.5 to 0.5
- up_offset: float32 [32], replicated, may hold values from -2.5 to 2.5
- conv_kernel: bfloat16 [32, 64, 3, 3, 3], replicated, may hold values from -0.15625 to 0.15625
- conv_bias: float32 [32], replicated, may hold values from -2.5 to 2.5
Outputs:
- level_output: bfloat16 [64, 16, 32, 128], P('groups', 'gx', 'gy'), parts along dimension 0
- skip_grad: bfloat16 [64, 16, 32, 128], P('groups', 'gx', 'gy'), parts along dimension 0
- kernel_grad: float32 [64, 64, 3, 3, 3], P('groups'), parts along dimension 0
- bias_grad: float32 [64], P('groups'), parts along dimension 0
- up_grad: float32 [64, 32, 3, 3, 3], P('groups'), parts along dimension 0
- offset_grad: float32 [64], P('groups'), parts along dimension 0
There are 2 independent parts, one for each index of `groups`. A program takes and returns all parts, laid end to end along the dimension named above; an argument that names none is the same for every part. Nothing has to cross between parts.
All inputs are finite; a program needn't handle non-finite values.
Results may differ from a plain program's by a relative error of at most 0.0049.
Values may be sent and summed in bfloat16 or wider, within the bound.
A program may use at most 64 MiB of HBM per device.

v0:
```python
import functools
import math

import jax
import jax.numpy as jnp
from jax import lax
from jax.experimental import pallas as pl
from jax.experimental.pallas import tpu as pltpu
from jax.sharding import PartitionSpec as P

f32 = jnp.float32
bf16 = jnp.bfloat16


def halo(block, axis, dim, low_width, high_width):
    count = lax.axis_size(axis)
    forward = [(i, (i + 1) % count) for i in range(count)]
    backward = [((i + 1) % count, i) for i in range(count)]
    extent = block.shape[dim]
    low = lax.ppermute(
        lax.slice_in_dim(block, extent - low_width, None, axis=dim), axis, forward
    )
    high = lax.ppermute(lax.slice_in_dim(block, 0, high_width, axis=dim), axis, backward)
    return jnp.concatenate([low, block, high], axis=dim)


def mm(lhs, rhs):
    return jnp.dot(lhs, rhs, preferred_element_type=f32)


def mmt(lhs, rhs):
    return lax.dot_general(lhs, rhs, (((1,), (1,)), ((), ())), preferred_element_type=f32)


def roll(value, shift):
    return pltpu.roll(value, shift % value.shape[-1], value.ndim - 1)


def body(dims, scaling, coarse, skip, cot, wee, weo, woe, woo, wf, wa, uo, cb,
         lvl, sg, tot, dil, joi, gra, gr3, uc3, akg, aug, abg, aog):
    ch, nx, ny, nz = dims
    hx, hy = nx // 2, ny // 2
    wide = (hy + 2) * nz
    spread = (
        lax.broadcasted_iota(jnp.int32, (nz // 2, nz), 1)
        == 2 * lax.broadcasted_iota(jnp.int32, (nz // 2, nz), 0)
    ).astype(f32).astype(bf16)
    for q in range(hy + 3):
        thin = mm(coarse[q], spread).astype(bf16)
        for p in range(hx + 3):
            dil[p, :, q * nz : (q + 1) * nz] = thin[p * ch : (p + 1) * ch]

    offset = jnp.broadcast_to(uo[...], (ch, nz))
    weights = ((wee, weo), (woe, woo))

    @pl.loop(0, hx + 2)
    def _(p):
        for px in range(2):
            for py in range(2):
                rhs = jnp.concatenate(
                    [
                        dil[p + ia, :, ib * nz : ib * nz + wide]
                        for ia in range(1 + px)
                        for ib in range(1 + py)
                    ],
                    axis=0,
                )
                t = mm(weights[px][py][...], rhs)
                for m in range(hy + 2):
                    s = slice(m * nz, (m + 1) * nz)
                    row = (
                        roll(t[:ch, s], -1) + t[ch : 2 * ch, s] + roll(t[2 * ch :, s], 1)
                    ) + offset
                    y = 2 * m + py
                    joi[2 * p + px, :ch, y * nz : (y + 1) * nz] = row.astype(bf16)
            joi[2 * p + px, ch:, :] = skip[2 * p + px]

    bias = jnp.broadcast_to(cb[...], (ch, nz))
    abg[...] = jnp.zeros_like(abg)
    aog[...] = jnp.zeros_like(aog)
    akg[...] = jnp.zeros_like(akg)
    aug[...] = jnp.zeros_like(aug)

    def forward(x, own):
        span = (ny + 2) * nz
        rhs = jnp.concatenate(
            [joi[x + a, :, b * nz : b * nz + span] for a in range(3) for b in range(3)], axis=0
        )
        t = mm(wf[...], rhs)
        for y in range(ny + 2):
            s = slice(y * nz, (y + 1) * nz)
            v = roll(t[:ch, s], 1) + t[ch : 2 * ch, s] + roll(t[2 * ch :, s], -1) + bias
            e = jnp.exp(jnp.minimum(v, 0.0))
            g = (cot[x, :, s].astype(f32) * jnp.where(v > 0.0, 1.0, e)).astype(bf16)
            gra[x, :, s] = g
            if own and 1 <= y <= ny:
                d = slice((y - 1) * nz, y * nz)
                lvl[x - 1, :, d] = jnp.where(v > 0.0, v, e - 1.0).astype(bf16)
                g = g.astype(f32)
                abg[...] += g
                gr3[x - 1, :ch, d] = roll(g, -1).astype(bf16)
                gr3[x - 1, ch : 2 * ch, d] = g.astype(bf16)
                gr3[x - 1, 2 * ch :, d] = roll(g, 1).astype(bf16)

    @pl.loop(0, 2)
    def _(i):
        forward(i * (nx + 1), False)

    @pl.loop(0, nx)
    def _(x):
        forward(x + 1, True)

    @pl.loop(0, nx)
    def _(x):
        span = ny * nz
        lhs = jnp.concatenate(
            [
                joi[x + 1 + a, :, (1 + b) * nz : (1 + b) * nz + span]
                for a in range(3)
                for b in range(3)
            ],
            axis=0,
        )
        akg[...] += mmt(lhs, gr3[x])

    @pl.loop(0, nx)
    def _(x):
        span = ny * nz
        rhs = jnp.concatenate(
            [gra[x + a, :, b * nz : b * nz + span] for a in range(3) for b in range(3)], axis=0
        )
        t = mm(wa[...], rhs)
        w = 2 * ch
        for y in range(ny):
            s = slice(y * nz, (y + 1) * nz)
            j = roll(t[:w, s], -1) + t[w : 2 * w, s] + roll(t[2 * w :, s], 1)
            sg[x, :, s] = j[ch:].astype(bf16)
            u = j[:ch].astype(bf16).astype(f32)
            aog[...] += u
            at = (y % 2) * hy + y // 2
            d = slice(at * nz, (at + 1) * nz)
            uc3[x, :ch, d] = roll(u, 1).astype(bf16)
            uc3[x, ch : 2 * ch, d] = u.astype(bf16)
            uc3[x, 2 * ch :, d] = roll(u, -1).astype(bf16)

    half = hy * nz
    taps = (((1, 0),), ((2, 0), (0, 1)))

    @pl.loop(0, hx)
    def _(p):
        for px in range(2):
            for py in range(2):
                lhs = jnp.concatenate(
                    [
                        dil[p + 1 + da, :, (1 + db) * nz : (1 + db) * nz + half]
                        for a, da in taps[px]
                        for b, db in taps[py]
                    ],
                    axis=0,
                )
                r = mmt(lhs, uc3[2 * p + px, :, py * half : (py + 1) * half])
                k = 0
                for a, da in taps[px]:
                    for b, db in taps[py]:
                        at = (a * 3 + b) * ch
                        aug[at : at + ch, :] += r[k : k + ch]
                        k += ch

    kg = akg[...].T * scaling
    ug = aug[...].T * scaling
    for ab in range(9):
        for c in range(3):
            o = slice(c * ch, (c + 1) * ch)
            tot[ab * 3 + c, :, : 2 * ch] = kg[o, ab * 2 * ch : (ab + 1) * 2 * ch]
            tot[ab * 3 + c, :, 2 * ch : 3 * ch] = ug[o, ab * ch : (ab + 1) * ch]
            tot[ab * 3 + c, :, 3 * ch :] = jnp.zeros((ch, ch), f32)
    bsum = jnp.sum(abg[...], axis=1, keepdims=True) * scaling
    osum = jnp.sum(aog[...], axis=1, keepdims=True) * scaling
    tot[27, :, : 2 * ch] = jnp.broadcast_to(bsum, (ch, 2 * ch))
    tot[27, :, 2 * ch :] = jnp.broadcast_to(osum, (ch, 2 * ch))


def local(coarse_field, skip_field, cotangent, up_kernel, up_offset, conv_kernel, conv_bias):
    ch, nx, ny, nz = skip_field.shape
    hx, hy = nx // 2, ny // 2
    cells = nx * ny * nz * lax.axis_size("gx") * lax.axis_size("gy")
    scaling = 1.0 / math.sqrt(cells)

    skip = jnp.transpose(skip_field, (1, 0, 2, 3)).reshape(nx, ch, ny * nz)
    cot = jnp.transpose(cotangent, (1, 0, 2, 3)).reshape(nx, ch, ny * nz)
    skip = halo(halo(skip, "gx", 0, 2, 2), "gy", 2, 2 * nz, 2 * nz)
    cot = halo(halo(cot, "gx", 0, 1, 1), "gy", 2, nz, nz)
    coarse = jnp.transpose(coarse_field, (2, 1, 0, 3))
    coarse = halo(halo(coarse, "gx", 1, 1, 2), "gy", 0, 1, 2)
    coarse = coarse.reshape(hy + 3, (hx + 3) * ch, nz // 2)

    def up_weight(taps_a, taps_b):
        w = jnp.stack([up_kernel[:, :, a, b, :] for a in taps_a for b in taps_b], axis=-1)
        return jnp.transpose(w, (2, 0, 3, 1)).reshape(3 * ch, -1)

    ups = [up_weight(a, b) for a in ((1,), (2, 0)) for b in ((1,), (2, 0))]
    wf = jnp.transpose(conv_kernel, (4, 0, 2, 3, 1)).reshape(3 * ch, 18 * ch)
    wa = jnp.transpose(conv_kernel[:, :, ::-1, ::-1, :], (4, 1, 2, 3, 0)).reshape(6 * ch, 9 * ch)

    vmem = pl.BlockSpec(memory_space=pltpu.VMEM)
    lvl, sg, tot = pl.pallas_call(
        functools.partial(body, (ch, nx, ny, nz), scaling),
        out_shape=(
            jax.ShapeDtypeStruct((nx, ch, ny * nz), bf16),
            jax.ShapeDtypeStruct((nx, ch, ny * nz), bf16),
            jax.ShapeDtypeStruct((28, ch, 4 * ch), f32),
        ),
        in_specs=[vmem] * 11,
        out_specs=(vmem, vmem, vmem),
        scratch_shapes=[
            pltpu.VMEM((hx + 3, ch, (hy + 3) * nz), bf16),
            pltpu.VMEM((nx + 4, 2 * ch, (ny + 4) * nz), bf16),
            pltpu.VMEM((nx + 2, ch, (ny + 2) * nz), bf16),
            pltpu.VMEM((nx, 3 * ch, ny * nz), bf16),
            pltpu.VMEM((nx, 3 * ch, ny * nz), bf16),
            pltpu.VMEM((18 * ch, 3 * ch), f32),
            pltpu.VMEM((9 * ch, 3 * ch), f32),
            pltpu.VMEM((ch, nz), f32),
            pltpu.VMEM((ch, nz), f32),
        ],
        compiler_params=pltpu.CompilerParams(vmem_limit_bytes=48 << 20),
        name="level",
    )(coarse, skip, cot, *ups, wf, wa, up_offset[:, None], conv_bias[:, None])

    tot = lax.psum(tot, ("gx", "gy"))

    def unpack(v):
        return jnp.transpose(v.reshape(nx, ch, ny, nz), (1, 0, 2, 3))

    def kernel_of(v):
        return jnp.transpose(v.reshape(3, 3, 3, ch, -1), (3, 4, 0, 1, 2))

    return (
        unpack(lvl),
        unpack(sg),
        kernel_of(tot[:27, :, : 2 * ch]),
        tot[27, :, 0],
        kernel_of(tot[:27, :, 2 * ch : 3 * ch]),
        tot[27, :, 2 * ch],
    )


def solution(mesh):
    field = P("groups", "gx", "gy", None)
    kernel = P("groups", None, None, None, None)
    return jax.shard_map(
        local,
        mesh=mesh,
        in_specs=(field, field, field, P(), P(), P(), P()),
        out_specs=(field, field, kernel, P("groups"), kernel, P("groups")),
        check_vma=False,
    )
```

profile of v0, /device:TPU:1, one launch (start us, length us, event | category | flops | bytes accessed | tf_op | source)
XLA Modules:
  0.0 151.0 jit_solution(9399424764771338404)
XLA Ops:
  7.3 0.8 slice.112
  8.1 2.7 %collective-permute-start = (bf16[4,1,32,64]{3,0,1,2:T(4,128)(2,1)S(1)}, bf16[4,1,32,64]{3,0,1,2:T(4,128)(2,1)S(1)}, u32[]{:S(2)}, u32[]{:S(2)}) collective-permute-start(bf16[4,1,32,64]{3,0,1,2:T(4,128)(2,1)S(1)} %slice.112), channel_id=1, source_target_pairs={{0,4},{4,8},{8,12},{12,0},{1,5},{5,9},{9,13},{13,1},{2,6},{6,10},{... | collective-permute-start | bytes 49160 | tf_op jit(solution)/shard_map/ppermute | solution.py:20
  10.8 0.9 fusion.2
  11.7 0.5 collective-permute-start.8
  12.4 1.0 fusion.3
  13.5 1.8 %collective-permute-start.4 = (bf16[2,32,1024]{2,1,0:T(8,128)(2,1)S(1)}, bf16[2,32,1024]{2,1,0:T(8,128)(2,1)S(1)}, u32[]{:S(2)}, u32[]{:S(2)}) collective-permute-start(bf16[2,32,1024]{2,1,0:T(8,128)(2,1)S(1)} %copy.42), channel_id=1, source_target_pairs={{0,4},{4,8},{8,12},{12,0},{1,5},{5,9},{9,13},{13,1},{2,6},{6,10},{... | collective-permute-start | bytes 393224 | tf_op jit(solution)/shard_map/ppermute | solution.py:20
  15.5 0.7 copy-done.3
  16.6 0.2 reshape.63
  17.7 0.2 reshape.62.wf
  18.5 1.3 collective-permute-start.2
  19.8 2.1 %collective-permute-start.3 = (bf16[2,5,32,64]{3,0,1,2:T(2,128)(2,1)S(1)}, bf16[2,5,32,64]{3,0,1,2:T(2,128)(2,1)S(1)}, u32[]{:S(2)}, u32[]{:S(2)}) collective-permute-start(bf16[2,5,32,64]{3,0,1,2:T(2,128)(2,1)S(1)} %slice.114), channel_id=1, source_target_pairs={{1,0},{2,1},{3,2},{0,3},{5,4},{6,5},{7,6},{4,7},{9,8},{10,9},{11,1... | collective-permute-start | bytes 122888 | tf_op jit(solution)/shard_map/ppermute | solution.py:23
  22.2 1.7 %collective-permute-done.2 = bf16[1,5,32,64]{3,0,1,2:T(2,128)(2,1)S(1)} collective-permute-done((bf16[1,5,32,64]{3,0,1,2:T(2,128)(2,1)S(1)}, bf16[1,5,32,64]{3,0,1,2:T(2,128)(2,1)S(1)}, u32[]{:S(2)}, u32[]{:S(2)}) %collective-permute-start.2) | collective-permute-done | bytes 20512 | tf_op jit(solution)/shard_map/ppermute | solution.py:20
  23.8 1.6 %collective-permute-start.11 = (bf16[6,32,128]{2,1,0:T(8,128)(2,1)S(1)}, bf16[6,32,128]{2,1,0:T(8,128)(2,1)S(1)}, u32[]{:S(2)}, u32[]{:S(2)}) collective-permute-start(bf16[6,32,128]{2,1,0:T(8,128)(2,1)S(1)} %get-tuple-element.17), channel_id=1, source_target_pairs={{1,0},{2,1},{3,2},{0,3},{5,4},{6,5},{7,6},{4,7},{9,8},{10,9},{11,1... | collective-permute-start | bytes 147464 | tf_op jit(solution)/shard_map/ppermute | solution.py:23
  25.4 0.3 pad_maximum_fusion.2
  26.0 0.4 collective-permute-start.6
  26.4 2.9 %collective-permute-start.7 = (bf16[8,32,256]{2,1,0:T(8,128)(2,1)S(1)}, bf16[8,32,256]{2,1,0:T(8,128)(2,1)S(1)}, u32[]{:S(2)}, u32[]{:S(2)}) collective-permute-start(bf16[8,32,256]{2,1,0:T(8,128)(2,1)S(1)} %get-tuple-element.15), channel_id=1, source_target_pairs={{1,0},{2,1},{3,2},{0,3},{5,4},{6,5},{7,6},{4,7},{9,8},{10,9},{11,1... | collective-permute-start | bytes 393224 | tf_op jit(solution)/shard_map/ppermute | solution.py:23
  29.4 2.8 %collective-permute-done.6 = bf16[8,32,256]{2,1,0:T(8,128)(2,1)S(1)} collective-permute-done((bf16[8,32,256]{2,1,0:T(8,128)(2,1)S(1)}, bf16[8,32,256]{2,1,0:T(8,128)(2,1)S(1)}, u32[]{:S(2)}, u32[]{:S(2)}) %collective-permute-start.6) | collective-permute-done | bytes 131104 | tf_op jit(solution)/shard_map/ppermute | solution.py:20
  32.3 11.0 %level.1 = (bf16[4,32,1024]{2,1,0:T(8,128)(2,1)S(1)}, bf16[4,32,1024]{2,1,0:T(8,128)(2,1)S(1)}, f32[28,32,128]{2,1,0:T(8,128)}) custom-call(bf16[7,160,64]{2,1,0:T(8,128)(2,1)S(1)} %bitcast.88, bf16[8,32,1536]{2,1,0:T(8,128)(2,1)S(1)} %pad_maximum_fusion.skip, bf16[6,32,1280]{2,1,0:T(8,128)(2,1)S(1)} %pad_maximum_fusion.1.cot, bf16[96,32]{1,0:T(8,128)(2,1)S(1)} %bitcast.91, ...), custom_call_target="tpu_custom_call" | custom-call | tf_op jit(solution)/shard_map/level/pallas_call | solution.py:206
  43.3 0.8 copy_bitcast_fusion.1
  44.1 0.7 copy_bitcast_fusion
  44.9 95.0 %all-reduce.2.cloned.1.call-done = f32[28,32,128]{2,1,0:T(8,128)} async-done(((f32[28,32,128]{2,1,0:T(8,128)}), f32[28,32,128]{2,1,0:T(8,128)}) %all-reduce.2.cloned.1.call-update) | async-done | bytes 458768 | tf_op jit(solution)/shard_map/psum | solution.py:230
  139.8 1.6 %slice_reduce_fusion = (f32[32]{0:T(128)}, f32[32]{0:T(128)}) fusion(f32[28,32,128]{2,1,0:T(8,128)} %all-reduce.2.cloned.1.call-done), kind=kLoop, calls=%fused_computation.20 | loop fusion | bytes 512 | tf_op jit(solution)/shard_map/slice | solution.py:244
  141.4 2.0 %slice.125 = f32[27,32,32]{2,1,0:T(8,128)} slice(f32[28,32,128]{2,1,0:T(8,128)} %all-reduce.2.cloned.1.call-done), slice={[0:27], [0:32], [64:96]} | slice | bytes 221184 | tf_op jit(solution)/shard_map/slice | solution.py:243
  143.4 0.8 slice.123
  (70 shorter events, 2.9 us)
Async XLA Ops:
  7.2 132.7 %all-reduce.2.cloned.1.call-start = ((), (), s32[]{:S(2)}) async-start(), calls=%async_computation | async-start | bytes 917504 | tf_op jit(solution)/shard_map/psum | solution.py:230
  7.2 10.8 %collective-permute-start.1 = (bf16[4,2,32,64]{3,0,1,2:T(4,128)(2,1)}, bf16[4,2,32,64]{3,0,1,2:T(4,128)(2,1)S(1)}, u32[]{:S(2)}, u32[]{:S(2)}) collective-permute-start(bf16[4,2,32,64]{3,0,1,2:T(4,128)(2,1)} %bitcast.101), channel_id=1, source_target_pairs={{4,0},{8,4},{12,8},{0,12},{5,1},{9,5},{13,9},{1,13},{6,2},{10,6},{... | collective-permute-start | bytes 98312 | tf_op jit(solution)/shard_map/ppermute | solution.py:23
  8.1 9.8 %collective-permute-start = (bf16[4,1,32,64]{3,0,1,2:T(4,128)(2,1)S(1)}, bf16[4,1,32,64]{3,0,1,2:T(4,128)(2,1)S(1)}, u32[]{:S(2)}, u32[]{:S(2)}) collective-permute-start(bf16[4,1,32,64]{3,0,1,2:T(4,128)(2,1)S(1)} %slice.112), channel_id=1, source_target_pairs={{0,4},{4,8},{8,12},{12,0},{1,5},{5,9},{9,13},{13,1},{2,6},{6,10},{... | collective-permute-start | bytes 49160 | tf_op jit(solution)/shard_map/ppermute | solution.py:20
  10.8 4.5 %copy-start.2 = (bf16[32,64,3,3,3]{1,0,4,3,2:T(8,128)(2,1)S(1)}, bf16[32,64,3,3,3]{1,0,4,3,2:T(8,128)(2,1)}, u32[]{:S(2)}) copy-start(bf16[32,64,3,3,3]{1,0,4,3,2:T(8,128)(2,1)} %param.12) | copy-start | bytes 331780
  11.7 8.1 %collective-permute-start.8 = (bf16[1,32,1024]{2,1,0:T(8,128)(2,1)S(1)}, bf16[1,32,1024]{2,1,0:T(8,128)(2,1)S(1)}, u32[]{:S(2)}, u32[]{:S(2)}) collective-permute-start(bf16[1,32,1024]{2,1,0:T(8,128)(2,1)S(1)} %slice.94), channel_id=1, source_target_pairs={{0,4},{4,8},{8,12},{12,0},{1,5},{5,9},{9,13},{13,1},{2,6},{6,10},{... | collective-permute-start | bytes 196616 | tf_op jit(solution)/shard_map/ppermute | solution.py:20
  12.2 3.0 %copy-start.5 = (bf16[32,32,3,3,3]{1,0,4,3,2:T(8,128)(2,1)S(1)}, bf16[32,32,3,3,3]{1,0,4,3,2:T(8,128)(2,1)}, u32[]{:S(2)}) copy-start(bf16[32,32,3,3,3]{1,0,4,3,2:T(8,128)(2,1)} %param.10) | copy-start | bytes 165892
  12.3 9.8 %collective-permute-start.9 = (bf16[1,32,1024]{2,1,0:T(8,128)(2,1)S(1)}, bf16[1,32,1024]{2,1,0:T(8,128)(2,1)S(1)}, u32[]{:S(2)}, u32[]{:S(2)}) collective-permute-start(bf16[1,32,1024]{2,1,0:T(8,128)(2,1)S(1)} %slice.96), channel_id=1, source_target_pairs={{4,0},{8,4},{12,8},{0,12},{5,1},{9,5},{13,9},{1,13},{6,2},{10,6},{... | collective-permute-start | bytes 196616 | tf_op jit(solution)/shard_map/ppermute | solution.py:23
  13.4 2.0 %copy-start.1 = (bf16[32,4,8,128]{3,2,1,0:T(8,128)(2,1)S(1)}, bf16[32,4,8,128]{3,2,1,0:T(8,128)(2,1)}, u32[]{:S(2)}) copy-start(bf16[32,4,8,128]{3,2,1,0:T(8,128)(2,1)} %param.8) | copy-start | bytes 786436
  13.5 12.4 %collective-permute-start.4 = (bf16[2,32,1024]{2,1,0:T(8,128)(2,1)S(1)}, bf16[2,32,1024]{2,1,0:T(8,128)(2,1)S(1)}, u32[]{:S(2)}, u32[]{:S(2)}) collective-permute-start(bf16[2,32,1024]{2,1,0:T(8,128)(2,1)S(1)} %copy.42), channel_id=1, source_target_pairs={{0,4},{4,8},{8,12},{12,0},{1,5},{5,9},{9,13},{13,1},{2,6},{6,10},{... | collective-permute-start | bytes 393224 | tf_op jit(solution)/shard_map/ppermute | solution.py:20
  15.2 1.0 copy-start.3
  15.3 1.0 copy-start.6
  15.3 1.1 copy-start.7
  17.3 0.8 copy-start.4
  17.9 8.0 %collective-permute-start.5 = (bf16[2,32,1024]{2,1,0:T(8,128)(2,1)S(1)}, bf16[2,32,1024]{2,1,0:T(8,128)(2,1)S(1)}, u32[]{:S(2)}, u32[]{:S(2)}) collective-permute-start(bf16[2,32,1024]{2,1,0:T(8,128)(2,1)S(1)} %copy.44), channel_id=1, source_target_pairs={{4,0},{8,4},{12,8},{0,12},{5,1},{9,5},{13,9},{1,13},{6,2},{10,6},{... | collective-permute-start | bytes 393224 | tf_op jit(solution)/shard_map/ppermute | solution.py:23
  18.5 5.3 %collective-permute-start.2 = (bf16[1,5,32,64]{3,0,1,2:T(2,128)(2,1)S(1)}, bf16[1,5,32,64]{3,0,1,2:T(2,128)(2,1)S(1)}, u32[]{:S(2)}, u32[]{:S(2)}) collective-permute-start(bf16[1,5,32,64]{3,0,1,2:T(2,128)(2,1)S(1)} %slice.113), channel_id=1, source_target_pairs={{0,1},{1,2},{2,3},{3,0},{4,5},{5,6},{6,7},{7,4},{8,9},{9,10},{10,1... | collective-permute-start | bytes 61448 | tf_op jit(solution)/shard_map/ppermute | solution.py:20
  19.8 5.6 %collective-permute-start.3 = (bf16[2,5,32,64]{3,0,1,2:T(2,128)(2,1)S(1)}, bf16[2,5,32,64]{3,0,1,2:T(2,128)(2,1)S(1)}, u32[]{:S(2)}, u32[]{:S(2)}) collective-permute-start(bf16[2,5,32,64]{3,0,1,2:T(2,128)(2,1)S(1)} %slice.114), channel_id=1, source_target_pairs={{1,0},{2,1},{3,2},{0,3},{5,4},{6,5},{7,6},{4,7},{9,8},{10,9},{11,1... | collective-permute-start | bytes 122888 | tf_op jit(solution)/shard_map/ppermute | solution.py:23
  22.1 7.2 %collective-permute-start.10 = (bf16[6,32,128]{2,1,0:T(8,128)(2,1)S(1)}, bf16[6,32,128]{2,1,0:T(8,128)(2,1)S(1)}, u32[]{:S(2)}, u32[]{:S(2)}) collective-permute-start(bf16[6,32,128]{2,1,0:T(8,128)(2,1)S(1)} %get-tuple-element.16), channel_id=1, source_target_pairs={{0,1},{1,2},{2,3},{3,0},{4,5},{5,6},{6,7},{7,4},{8,9},{9,10},{10,1... | collective-permute-start | bytes 147464 | tf_op jit(solution)/shard_map/ppermute | solution.py:20
  23.8 5.5 %collective-permute-start.11 = (bf16[6,32,128]{2,1,0:T(8,128)(2,1)S(1)}, bf16[6,32,128]{2,1,0:T(8,128)(2,1)S(1)}, u32[]{:S(2)}, u32[]{:S(2)}) collective-permute-start(bf16[6,32,128]{2,1,0:T(8,128)(2,1)S(1)} %get-tuple-element.17), channel_id=1, source_target_pairs={{1,0},{2,1},{3,2},{0,3},{5,4},{6,5},{7,6},{4,7},{9,8},{10,9},{11,1... | collective-permute-start | bytes 147464 | tf_op jit(solution)/shard_map/ppermute | solution.py:23
  26.0 6.2 %collective-permute-start.6 = (bf16[8,32,256]{2,1,0:T(8,128)(2,1)S(1)}, bf16[8,32,256]{2,1,0:T(8,128)(2,1)S(1)}, u32[]{:S(2)}, u32[]{:S(2)}) collective-permute-start(bf16[8,32,256]{2,1,0:T(8,128)(2,1)S(1)} %get-tuple-element.14), channel_id=1, source_target_pairs={{0,1},{1,2},{2,3},{3,0},{4,5},{5,6},{6,7},{7,4},{8,9},{9,10},{10,1... | collective-permute-start | bytes 393224 | tf_op jit(solution)/shard_map/ppermute | solution.py:20
  26.4 5.8 %collective-permute-start.7 = (bf16[8,32,256]{2,1,0:T(8,128)(2,1)S(1)}, bf16[8,32,256]{2,1,0:T(8,128)(2,1)S(1)}, u32[]{:S(2)}, u32[]{:S(2)}) collective-permute-start(bf16[8,32,256]{2,1,0:T(8,128)(2,1)S(1)} %get-tuple-element.15), channel_id=1, source_target_pairs={{1,0},{2,1},{3,2},{0,3},{5,4},{6,5},{7,6},{4,7},{9,8},{10,9},{11,1... | collective-permute-start | bytes 393224 | tf_op jit(solution)/shard_map/ppermute | solution.py:23
  139.8 3.5 %copy-start = (f32[28,32,128]{2,1,0:T(8,128)S(1)}, f32[28,32,128]{2,1,0:T(8,128)}, u32[]{:S(2)}) copy-start(f32[28,32,128]{2,1,0:T(8,128)} %all-reduce.2.cloned.1.call-done) | copy-start | bytes 1376260
Sparse Core Ops, SparseCore 0:
  44.2 95.5 all-reduce.1
where the time goes:
time: 151 us
  waiting for transfers between devices  99.5 us (66%)
  between operations  14.4 us (10%)
  starting transfers between devices  13.7 us (9%)
  local copies, waits for them, and re-layouts  11.8 us (8%)
  Pallas kernels  11 us (7%)
    psum x1, waiting for transfers between devices, local(): tot = lax.psum(tot, ('gx', 'gy'))  95 us
    pallas_call x1, Pallas kernels, local(): pl.pallas_call(functools.partial(body, (ch, nx, ny, nz), scaling), out_sh...  11 us
    ppermute x6, starting transfers between devices, halo(): lax.ppermute(lax.slice_in_dim(block, 0, high_width, axis=dim), axis, back...  6.83 us
    ppermute x6, starting transfers between devices, halo(): lax.ppermute(lax.slice_in_dim(block, extent - low_width, None, axis=dim),...  6.8 us
    ppermute x6, waiting for transfers between devices, halo(): lax.ppermute(lax.slice_in_dim(block, extent - low_width, None, axis=dim),...  4.48 us
  transfers between devices with their start and end apart: 13, of which 3 were waited for; matrix products, arithmetic and copies ran while one was open for 4% of the time, Pallas kernels for 0%

commit v1 on v0

--- a/solution.py
+++ b/solution.py
@@ -171,13 +171,103 @@
     for ab in range(9):
         for c in range(3):
             o = slice(c * ch, (c + 1) * ch)
-            tot[ab * 3 + c, :, : 2 * ch] = kg[o, ab * 2 * ch : (ab + 1) * 2 * ch]
-            tot[ab * 3 + c, :, 2 * ch : 3 * ch] = ug[o, ab * ch : (ab + 1) * ch]
-            tot[ab * 3 + c, :, 3 * ch :] = jnp.zeros((ch, ch), f32)
-    bsum = jnp.sum(abg[...], axis=1, keepdims=True) * scaling
-    osum = jnp.sum(aog[...], axis=1, keepdims=True) * scaling
-    tot[27, :, : 2 * ch] = jnp.broadcast_to(bsum, (ch, 2 * ch))
-    tot[27, :, 2 * ch :] = jnp.broadcast_to(osum, (ch, 2 * ch))
+            d = slice((ab * 3 + c) * ch, (ab * 3 + c + 1) * ch)
+            tot[d, : 2 * ch] = kg[o, ab * 2 * ch : (ab + 1) * 2 * ch]
+            tot[d, 2 * ch : 3 * ch] = ug[o, ab * ch : (ab + 1) * ch]
+            tot[d, 3 * ch :] = jnp.zeros((ch, ch), f32)
+    tot[27 * ch :, :] = jnp.zeros((tot.shape[0] - 27 * ch, tot.shape[1]), f32)
+    tot[27 * ch : 27 * ch + 1, :ch] = jnp.sum(abg[...].T, axis=0, keepdims=True) * scaling
+    tot[27 * ch + 8 : 27 * ch + 9, :ch] = jnp.sum(aog[...].T, axis=0, keepdims=True) * scaling
+
+
+def partners(axis):
+    me, count = lax.axis_index(axis), lax.axis_size(axis)
+    return me, [lax.rem(me + d, count) for d in range(1, count)]
+
+
+def reduce_body(ch, part, kg, bg, ug, og, land_x, own, land_y, res, send, recv):
+    me_x, to_x = partners("gx")
+    me_y, to_y = partners("gy")
+    barrier = pltpu.get_barrier_semaphore()
+    for axis, to in (("gx", to_x), ("gy", to_y)):
+        for i in to:
+            pl.semaphore_signal(
+                barrier, inc=1, device_id={axis: i}, device_id_type=pl.DeviceIdType.MESH
+            )
+    pl.semaphore_wait(barrier, len(to_x) + len(to_y))
+    used = [0]
+
+    def copy(src, dst, axis, i):
+        k = used[0]
+        used[0] += 1
+        c = pltpu.make_async_remote_copy(
+            src_ref=src,
+            dst_ref=dst,
+            send_sem=send.at[k],
+            recv_sem=recv.at[k],
+            device_id={axis: i},
+            device_id_type=pl.DeviceIdType.MESH,
+        )
+        c.start()
+        return c
+
+    started = []
+
+    def settle(copies):
+        started.extend(copies)
+        for c in copies:
+            c.wait_recv()
+
+    settle([copy(part.at[i], land_x.at[d], "gx", i) for d, i in enumerate(to_x)])
+    total = part[me_x]
+    for d in range(len(to_x)):
+        total = total + land_x[d]
+    own[...] = total
+    settle([copy(own.at[j], land_y.at[d], "gy", j) for d, j in enumerate(to_y)])
+    total = own[me_y]
+    for d in range(len(to_y)):
+        total = total + land_y[d]
+    res[me_x, me_y] = total
+    settle([copy(res.at[me_x, me_y], res.at[me_x, me_y], "gy", j) for j in to_y])
+    settle([copy(res.at[me_x], res.at[me_x], "gx", i) for i in to_x])
+    full = res[...].reshape(-1, res.shape[-1])
+    taps = full[: 27 * ch].reshape(27, ch, -1)
+    kg[...] = taps[:, :, : 2 * ch]
+    ug[...] = taps[:, :, 2 * ch : 3 * ch]
+    bg[...] = full[27 * ch : 27 * ch + 1, :ch]
+    og[...] = full[27 * ch + 8 : 27 * ch + 9, :ch]
+    for c in started:
+        c.wait_send()
+
+
+def all_sum(tot, ch):
+    gx, gy = lax.axis_size("gx"), lax.axis_size("gy")
+    rows, lanes = tot.shape[0] // (gx * gy), tot.shape[1]
+    vmem = pl.BlockSpec(memory_space=pltpu.VMEM)
+    copies = 2 * (gx - 1) + 2 * (gy - 1)
+    return pl.pallas_call(
+        functools.partial(reduce_body, ch),
+        out_shape=(
+            jax.ShapeDtypeStruct((27, ch, 2 * ch), f32),
+            jax.ShapeDtypeStruct((1, ch), f32),
+            jax.ShapeDtypeStruct((27, ch, ch), f32),
+            jax.ShapeDtypeStruct((1, ch), f32),
+        ),
+        in_specs=[vmem],
+        out_specs=(vmem,) * 4,
+        scratch_shapes=[
+            pltpu.VMEM((gx - 1, gy, rows, lanes), f32),
+            pltpu.VMEM((gy, rows, lanes), f32),
+            pltpu.VMEM((gy - 1, rows, lanes), f32),
+            pltpu.VMEM((gx, gy, rows, lanes), f32),
+            pltpu.SemaphoreType.DMA((copies,)),
+            pltpu.SemaphoreType.DMA((copies,)),
+        ],
+        compiler_params=pltpu.CompilerParams(
+            collective_id=1, has_side_effects=True, vmem_limit_bytes=32 << 20
+        ),
+        name="total",
+    )(tot.reshape(gx, gy, rows, lanes))
 
 
 def local(coarse_field, skip_field, cotangent, up_kernel, up_offset, conv_kernel, conv_bias):
@@ -202,13 +292,15 @@
     wf = jnp.transpose(conv_kernel, (4, 0, 2, 3, 1)).reshape(3 * ch, 18 * ch)
     wa = jnp.transpose(conv_kernel[:, :, ::-1, ::-1, :], (4, 1, 2, 3, 0)).reshape(6 * ch, 9 * ch)
 
+    parts = lax.axis_size("gx") * lax.axis_size("gy")
+    rows = 8 * parts * pl.cdiv(28 * ch, 8 * parts)
     vmem = pl.BlockSpec(memory_space=pltpu.VMEM)
     lvl, sg, tot = pl.pallas_call(
         functools.partial(body, (ch, nx, ny, nz), scaling),
         out_shape=(
             jax.ShapeDtypeStruct((nx, ch, ny * nz), bf16),
             jax.ShapeDtypeStruct((nx, ch, ny * nz), bf16),
-            jax.ShapeDtypeStruct((28, ch, 4 * ch), f32),
+            jax.ShapeDtypeStruct((rows, 4 * ch), f32),
         ),
         in_specs=[vmem] * 11,
         out_specs=(vmem, vmem, vmem),
@@ -227,7 +319,7 @@
         name="level",
     )(coarse, skip, cot, *ups, wf, wa, up_offset[:, None], conv_bias[:, None])
 
-    tot = lax.psum(tot, ("gx", "gy"))
+    kg, bg, ug, og = all_sum(tot, ch)
 
     def unpack(v):
         return jnp.transpose(v.reshape(nx, ch, ny, nz), (1, 0, 2, 3))
@@ -238,10 +330,10 @@
     return (
         unpack(lvl),
         unpack(sg),
-        kernel_of(tot[:27, :, : 2 * ch]),
-        tot[27, :, 0],
-        kernel_of(tot[:27, :, 2 * ch : 3 * ch]),
-        tot[27, :, 2 * ch],
+        kernel_of(kg),
+        bg.reshape(ch),
+        kernel_of(ug),
+        og.reshape(ch),
     )
 
 

time: 151 us -> 67.5 us (0.45)
  waiting for transfers between devices: 99.5 us -> 4.49 us
  Pallas kernels: 11 us -> 37.4 us
  between operations: 14.4 us -> 1.02 us
  local copies, waits for them, and re-layouts: 11.8 us -> 10 us
    psum x1 -> x0, waiting for transfers between devices: 95 us -> none  [local(): tot = lax.psum(tot, ('gx', 'gy'))]
    pallas_call x0 -> x1, Pallas kernels: none -> 27.3 us  [all_sum(): pl.pallas_call(functools.partial(reduce_body, ch), out_shape=(jax.ShapeDt...]
    slice x3 -> x0, local copies, waits for them, and re-layouts: 4.31 us -> none  [the longest x1 1.96 us: local(): tot[:27, :, 2 * ch:3 * ch]]
    unnamed x22 -> x24, local copies, waits for them, and re-layouts: 1.23 us -> 3.78 us
  transfers between devices with their start and end apart: 13 -> 12, of which waited for: 3 -> 2; matrix products, arithmetic and copies ran while one was open for 4% -> 8% of each run, Pallas kernels for 0% -> 0%
where the time goes in v1:
time: 67.5 us; the launch traced here: 67.3 us
  Pallas kernels  37.4 us (55%)
  starting transfers between devices  13.6 us (20%)
  local copies, waits for them, and re-layouts  10 us (15%)
  waiting for transfers between devices  4.49 us (7%)
  between operations  1.02 us (2%)
    pallas_call x1, Pallas kernels, all_sum(): pl.pallas_call(functools.partial(reduce_body, ch), out_shape=(jax.ShapeDt...  27.3 us
    pallas_call x1, Pallas kernels, local(): pl.pallas_call(functools.partial(body, (ch, nx, ny, nz), scaling), out_sh...  10.2 us
    ppermute x6, starting transfers between devices, halo(): lax.ppermute(lax.slice_in_dim(block, 0, high_width, axis=dim), axis, back...  6.83 us
    ppermute x6, starting transfers between devices, halo(): lax.ppermute(lax.slice_in_dim(block, extent - low_width, None, axis=dim),...  6.8 us
    ppermute x6, waiting for transfers between devices, halo(): lax.ppermute(lax.slice_in_dim(block, extent - low_width, None, axis=dim),...  4.48 us
    unnamed x24, local copies, waits for them, and re-layouts  3.78 us
    slice x6, local copies, waits for them, and re-layouts, halo(): lax.slice_in_dim(block, 0, high_width, axis=dim)  2.06 us
    transpose x2, local copies, waits for them, and re-layouts, unpack(): return jnp.transpose(v.reshape(nx, ch, ny, nz), (1, 0, 2, 3))  1.5 us
  transfers between devices with their start and end apart: 12, of which 2 were waited for; matrix products, arithmetic and copies ran while one was open for 8% of the time, Pallas kernels for 0%

profile of v1, /device:TPU:1, one launch (start us, length us, event | category | flops | bytes accessed | tf_op | source)
XLA Modules:
  0.0 67.3 jit_solution(17527355068962628135)
XLA Ops:
  0.7 0.8 %slice.96 = bf16[4,1,32,64]{3,0,1,2:T(4,128)(2,1)S(1)} slice(bf16[4,2,32,64]{3,0,1,2:T(4,128)(2,1)} %bitcast.108), slice={[0:4], [1:2], [0:32], [0:64]} | slice | bytes 32768 | tf_op jit(solution)/shard_map/slice | solution.py:21
  1.5 2.7 %collective-permute-start = (bf16[4,1,32,64]{3,0,1,2:T(4,128)(2,1)S(1)}, bf16[4,1,32,64]{3,0,1,2:T(4,128)(2,1)S(1)}, u32[]{:S(2)}, u32[]{:S(2)}) collective-permute-start(bf16[4,1,32,64]{3,0,1,2:T(4,128)(2,1)S(1)} %slice.96), channel_id=1, source_target_pairs={{0,4},{4,8},{8,12},{12,0},{1,5},{5,9},{9,13},{13,1},{2,6},{6,10},{... | collective-permute-start | bytes 49160 | tf_op jit(solution)/shard_map/ppermute | solution.py:20
  4.2 0.9 %fusion.2 = (bf16[1,32,8,128]{3,2,0,1:T(8,128)(2,1)S(1)}, bf16[1,32,8,128]{3,2,0,1:T(8,128)(2,1)S(1)}) fusion(bf16[4,32,8,128]{3,2,0,1:T(8,128)(2,1)} %bitcast.105), kind=kLoop, calls=%fused_computation.26 | loop fusion | bytes 262144 | tf_op jit(solution)/shard_map/slice | solution.py:23
  5.1 0.5 collective-permute-start.8
  5.8 1.0 %fusion.3 = (bf16[2,32,8,128]{3,2,0,1:T(8,128)(2,1)S(1)}, bf16[2,32,8,128]{3,2,0,1:T(8,128)(2,1)S(1)}) fusion(bf16[4,32,8,128]{3,2,0,1:T(8,128)(2,1)} %bitcast.100), kind=kLoop, calls=%fused_computation.27 | loop fusion | bytes 524288 | tf_op jit(solution)/shard_map/slice | solution.py:23
  6.9 1.8 %collective-permute-start.4 = (bf16[2,32,1024]{2,1,0:T(8,128)(2,1)S(1)}, bf16[2,32,1024]{2,1,0:T(8,128)(2,1)S(1)}, u32[]{:S(2)}, u32[]{:S(2)}) collective-permute-start(bf16[2,32,1024]{2,1,0:T(8,128)(2,1)S(1)} %copy.42), channel_id=1, source_target_pairs={{0,4},{4,8},{8,12},{12,0},{1,5},{5,9},{9,13},{13,1},{2,6},{6,10},{... | collective-permute-start | bytes 393224 | tf_op jit(solution)/shard_map/ppermute | solution.py:20
  8.9 0.7 %copy-done.2 = bf16[32,4,8,128]{3,2,1,0:T(8,128)(2,1)S(1)} copy-done((bf16[32,4,8,128]{3,2,1,0:T(8,128)(2,1)S(1)}, bf16[32,4,8,128]{3,2,1,0:T(8,128)(2,1)}, u32[]{:S(2)}) %copy-start.2) | copy-done | bytes 262168
  11.1 0.2 reshape.71.wf
  11.9 1.3 %collective-permute-start.2 = (bf16[1,5,32,64]{3,0,1,2:T(2,128)(2,1)S(1)}, bf16[1,5,32,64]{3,0,1,2:T(2,128)(2,1)S(1)}, u32[]{:S(2)}, u32[]{:S(2)}) collective-permute-start(bf16[1,5,32,64]{3,0,1,2:T(2,128)(2,1)S(1)} %slice.97), channel_id=1, source_target_pairs={{0,1},{1,2},{2,3},{3,0},{4,5},{5,6},{6,7},{7,4},{8,9},{9,10},{10,1... | collective-permute-start | bytes 61448 | tf_op jit(solution)/shard_map/ppermute | solution.py:20
  13.3 2.1 %collective-permute-start.3 = (bf16[2,5,32,64]{3,0,1,2:T(2,128)(2,1)S(1)}, bf16[2,5,32,64]{3,0,1,2:T(2,128)(2,1)S(1)}, u32[]{:S(2)}, u32[]{:S(2)}) collective-permute-start(bf16[2,5,32,64]{3,0,1,2:T(2,128)(2,1)S(1)} %slice.98), channel_id=1, source_target_pairs={{1,0},{2,1},{3,2},{0,3},{5,4},{6,5},{7,6},{4,7},{9,8},{10,9},{11,1... | collective-permute-start | bytes 122888 | tf_op jit(solution)/shard_map/ppermute | solution.py:23
  15.6 1.7 %collective-permute-done.2 = bf16[1,5,32,64]{3,0,1,2:T(2,128)(2,1)S(1)} collective-permute-done((bf16[1,5,32,64]{3,0,1,2:T(2,128)(2,1)S(1)}, bf16[1,5,32,64]{3,0,1,2:T(2,128)(2,1)S(1)}, u32[]{:S(2)}, u32[]{:S(2)}) %collective-permute-start.2) | collective-permute-done | bytes 20512 | tf_op jit(solution)/shard_map/ppermute | solution.py:20
  17.2 1.6 %collective-permute-start.11 = (bf16[6,32,128]{2,1,0:T(8,128)(2,1)S(1)}, bf16[6,32,128]{2,1,0:T(8,128)(2,1)S(1)}, u32[]{:S(2)}, u32[]{:S(2)}) collective-permute-start(bf16[6,32,128]{2,1,0:T(8,128)(2,1)S(1)} %get-tuple-element.23), channel_id=1, source_target_pairs={{1,0},{2,1},{3,2},{0,3},{5,4},{6,5},{7,6},{4,7},{9,8},{10,9},{11,1... | collective-permute-start | bytes 147464 | tf_op jit(solution)/shard_map/ppermute | solution.py:23
  18.8 0.3 pad_maximum_fusion.2
  19.4 0.4 collective-permute-start.6
  19.9 2.9 %collective-permute-start.7 = (bf16[8,32,256]{2,1,0:T(8,128)(2,1)S(1)}, bf16[8,32,256]{2,1,0:T(8,128)(2,1)S(1)}, u32[]{:S(2)}, u32[]{:S(2)}) collective-permute-start(bf16[8,32,256]{2,1,0:T(8,128)(2,1)S(1)} %get-tuple-element.21), channel_id=1, source_target_pairs={{1,0},{2,1},{3,2},{0,3},{5,4},{6,5},{7,6},{4,7},{9,8},{10,9},{11,1... | collective-permute-start | bytes 393224 | tf_op jit(solution)/shard_map/ppermute | solution.py:23
  22.8 2.8 %collective-permute-done.6 = bf16[8,32,256]{2,1,0:T(8,128)(2,1)S(1)} collective-permute-done((bf16[8,32,256]{2,1,0:T(8,128)(2,1)S(1)}, bf16[8,32,256]{2,1,0:T(8,128)(2,1)S(1)}, u32[]{:S(2)}, u32[]{:S(2)}) %collective-permute-start.6) | collective-permute-done | bytes 131104 | tf_op jit(solution)/shard_map/ppermute | solution.py:20
  25.7 10.2 %level.1 = (bf16[4,32,1024]{2,1,0:T(8,128)(2,1)S(1)}, bf16[4,32,1024]{2,1,0:T(8,128)(2,1)S(1)}, f32[896,128]{1,0:T(8,128)S(1)}) custom-call(bf16[7,160,64]{2,1,0:T(8,128)(2,1)S(1)} %bitcast.91, bf16[8,32,1536]{2,1,0:T(8,128)(2,1)S(1)} %pad_maximum_fusion.skip, bf16[6,32,1280]{2,1,0:T(8,128)(2,1)S(1)} %pad_maximum_fusion.1.cot, bf16[96,32]{1,0:T(8,128)(2,1)S(1)} %bitcast.97, ...), custom_call_target="tpu_custom_call" | custom-call | tf_op jit(solution)/shard_map/level/pallas_call | solution.py:298
  35.9 0.8 %copy_bitcast_fusion.1 = bf16[32,4,8,128]{3,2,1,0:T(8,128)(2,1)} fusion(bf16[4,32,8,128]{3,2,1,0:T(8,128)(2,1)S(1)} %bitcast.102), kind=kLoop, calls=%fused_computation.6 | loop fusion | bytes 524288 | tf_op jit(solution)/shard_map/transpose | solution.py:325
  36.7 0.8 %copy_bitcast_fusion = bf16[32,4,8,128]{3,2,1,0:T(8,128)(2,1)} fusion(bf16[4,32,8,128]{3,2,1,0:T(8,128)(2,1)S(1)} %bitcast.103), kind=kLoop, calls=%fused_computation.5 | loop fusion | bytes 524288 | tf_op jit(solution)/shard_map/transpose | solution.py:325
  37.5 27.3 %total.1 = (f32[27,32,64]{2,1,0:T(8,128)S(1)}, f32[1,32]{1,0:T(1,128)S(1)}, f32[27,32,32]{2,1,0:T(8,128)S(1)}, f32[1,32]{1,0:T(1,128)S(1)}) custom-call(f32[4,4,56,128]{3,2,1,0:T(8,128)S(1)} %bitcast.92), custom_call_target="tpu_custom_call" | custom-call | tf_op jit(solution)/shard_map/total/pallas_call | solution.py:248
  64.7 0.8 %copy.60 = f32[32,64,3,3,3]{1,0,4,3,2:T(8,128)} copy(f32[32,64,3,3,3]{1,0,4,3,2:T(8,128)S(1)} %bitcast.94) | data formatting | bytes 442368
  65.5 0.5 copy.61
  66.0 0.8 %copy.62 = f32[32,32,3,3,3]{1,0,4,3,2:T(8,128)} copy(f32[32,32,3,3,3]{1,0,4,3,2:T(8,128)S(1)} %bitcast.93) | data formatting | bytes 221184
  66.8 0.5 copy.63
  (67 shorter events, 3.0 us)
Async XLA Ops:
  0.6 10.8 %collective-permute-start.1 = (bf16[4,2,32,64]{3,0,1,2:T(4,128)(2,1)}, bf16[4,2,32,64]{3,0,1,2:T(4,128)(2,1)S(1)}, u32[]{:S(2)}, u32[]{:S(2)}) collective-permute-start(bf16[4,2,32,64]{3,0,1,2:T(4,128)(2,1)} %bitcast.107), channel_id=1, source_target_pairs={{4,0},{8,4},{12,8},{0,12},{5,1},{9,5},{13,9},{1,13},{6,2},{10,6},{... | collective-permute-start | bytes 98312 | tf_op jit(solution)/shard_map/ppermute | solution.py:23
  1.5 9.8 %collective-permute-start = (bf16[4,1,32,64]{3,0,1,2:T(4,128)(2,1)S(1)}, bf16[4,1,32,64]{3,0,1,2:T(4,128)(2,1)S(1)}, u32[]{:S(2)}, u32[]{:S(2)}) collective-permute-start(bf16[4,1,32,64]{3,0,1,2:T(4,128)(2,1)S(1)} %slice.96), channel_id=1, source_target_pairs={{0,4},{4,8},{8,12},{12,0},{1,5},{5,9},{9,13},{13,1},{2,6},{6,10},{... | collective-permute-start | bytes 49160 | tf_op jit(solution)/shard_map/ppermute | solution.py:20
  4.2 4.5 %copy-start.1 = (bf16[32,64,3,3,3]{1,0,4,3,2:T(8,128)(2,1)S(1)}, bf16[32,64,3,3,3]{1,0,4,3,2:T(8,128)(2,1)}, u32[]{:S(2)}) copy-start(bf16[32,64,3,3,3]{1,0,4,3,2:T(8,128)(2,1)} %param.12) | copy-start | bytes 331780
  5.1 8.1 %collective-permute-start.8 = (bf16[1,32,1024]{2,1,0:T(8,128)(2,1)S(1)}, bf16[1,32,1024]{2,1,0:T(8,128)(2,1)S(1)}, u32[]{:S(2)}, u32[]{:S(2)}) collective-permute-start(bf16[1,32,1024]{2,1,0:T(8,128)(2,1)S(1)} %slice.82), channel_id=1, source_target_pairs={{0,4},{4,8},{8,12},{12,0},{1,5},{5,9},{9,13},{13,1},{2,6},{6,10},{... | collective-permute-start | bytes 196616 | tf_op jit(solution)/shard_map/ppermute | solution.py:20
  5.7 3.0 %copy-start.4 = (bf16[32,32,3,3,3]{1,0,4,3,2:T(8,128)(2,1)S(1)}, bf16[32,32,3,3,3]{1,0,4,3,2:T(8,128)(2,1)}, u32[]{:S(2)}) copy-start(bf16[32,32,3,3,3]{1,0,4,3,2:T(8,128)(2,1)} %param.10) | copy-start | bytes 165892
  5.7 9.8 %collective-permute-start.9 = (bf16[1,32,1024]{2,1,0:T(8,128)(2,1)S(1)}, bf16[1,32,1024]{2,1,0:T(8,128)(2,1)S(1)}, u32[]{:S(2)}, u32[]{:S(2)}) collective-permute-start(bf16[1,32,1024]{2,1,0:T(8,128)(2,1)S(1)} %slice.84), channel_id=1, source_target_pairs={{4,0},{8,4},{12,8},{0,12},{5,1},{9,5},{13,9},{1,13},{6,2},{10,6},{... | collective-permute-start | bytes 196616 | tf_op jit(solution)/shard_map/ppermute | solution.py:23
  6.8 2.0 %copy-start = (bf16[32,4,8,128]{3,2,1,0:T(8,128)(2,1)S(1)}, bf16[32,4,8,128]{3,2,1,0:T(8,128)(2,1)}, u32[]{:S(2)}) copy-start(bf16[32,4,8,128]{3,2,1,0:T(8,128)(2,1)} %param.8) | copy-start | bytes 786436
  6.9 12.4 %collective-permute-start.4 = (bf16[2,32,1024]{2,1,0:T(8,128)(2,1)S(1)}, bf16[2,32,1024]{2,1,0:T(8,128)(2,1)S(1)}, u32[]{:S(2)}, u32[]{:S(2)}) collective-permute-start(bf16[2,32,1024]{2,1,0:T(8,128)(2,1)S(1)} %copy.42), channel_id=1, source_target_pairs={{0,4},{4,8},{8,12},{12,0},{1,5},{5,9},{9,13},{13,1},{2,6},{6,10},{... | collective-permute-start | bytes 393224 | tf_op jit(solution)/shard_map/ppermute | solution.py:20
  8.7 1.0 %copy-start.2 = (bf16[32,4,8,128]{3,2,1,0:T(8,128)(2,1)S(1)}, bf16[32,4,8,128]{3,2,1,0:T(8,128)(2,1)}, u32[]{:S(2)}) copy-start(bf16[32,4,8,128]{3,2,1,0:T(8,128)(2,1)} %param.9) | copy-start | bytes 786436
  8.7 1.0 %copy-start.5 = (f32[32]{0:T(128)S(1)}, f32[32]{0:T(128)}, u32[]{:S(2)}) copy-start(f32[32]{0:T(128)} %param.11) | copy-start | bytes 388
  8.7 1.1 %copy-start.6 = (f32[32]{0:T(128)S(1)}, f32[32]{0:T(128)}, u32[]{:S(2)}) copy-start(f32[32]{0:T(128)} %param.13) | copy-start | bytes 388
  10.8 0.8 %copy-start.3 = (bf16[32,2,4,64]{3,2,1,0:T(4,128)(2,1)S(1)}, bf16[32,2,4,64]{3,2,1,0:T(4,128)(2,1)}, u32[]{:S(2)}) copy-start(bf16[32,2,4,64]{3,2,1,0:T(4,128)(2,1)} %param.7) | copy-start | bytes 98308
  11.3 8.0 %collective-permute-start.5 = (bf16[2,32,1024]{2,1,0:T(8,128)(2,1)S(1)}, bf16[2,32,1024]{2,1,0:T(8,128)(2,1)S(1)}, u32[]{:S(2)}, u32[]{:S(2)}) collective-permute-start(bf16[2,32,1024]{2,1,0:T(8,128)(2,1)S(1)} %copy.44), channel_id=1, source_target_pairs={{4,0},{8,4},{12,8},{0,12},{5,1},{9,5},{13,9},{1,13},{6,2},{10,6},{... | collective-permute-start | bytes 393224 | tf_op jit(solution)/shard_map/ppermute | solution.py:23
  11.9 5.3 %collective-permute-start.2 = (bf16[1,5,32,64]{3,0,1,2:T(2,128)(2,1)S(1)}, bf16[1,5,32,64]{3,0,1,2:T(2,128)(2,1)S(1)}, u32[]{:S(2)}, u32[]{:S(2)}) collective-permute-start(bf16[1,5,32,64]{3,0,1,2:T(2,128)(2,1)S(1)} %slice.97), channel_id=1, source_target_pairs={{0,1},{1,2},{2,3},{3,0},{4,5},{5,6},{6,7},{7,4},{8,9},{9,10},{10,1... | collective-permute-start | bytes 61448 | tf_op jit(solution)/shard_map/ppermute | solution.py:20
  13.3 5.6 %collective-permute-start.3 = (bf16[2,5,32,64]{3,0,1,2:T(2,128)(2,1)S(1)}, bf16[2,5,32,64]{3,0,1,2:T(2,128)(2,1)S(1)}, u32[]{:S(2)}, u32[]{:S(2)}) collective-permute-start(bf16[2,5,32,64]{3,0,1,2:T(2,128)(2,1)S(1)} %slice.98), channel_id=1, source_target_pairs={{1,0},{2,1},{3,2},{0,3},{5,4},{6,5},{7,6},{4,7},{9,8},{10,9},{11,1... | collective-permute-start | bytes 122888 | tf_op jit(solution)/shard_map/ppermute | solution.py:23
  15.5 7.2 %collective-permute-start.10 = (bf16[6,32,128]{2,1,0:T(8,128)(2,1)S(1)}, bf16[6,32,128]{2,1,0:T(8,128)(2,1)S(1)}, u32[]{:S(2)}, u32[]{:S(2)}) collective-permute-start(bf16[6,32,128]{2,1,0:T(8,128)(2,1)S(1)} %get-tuple-element.22), channel_id=1, source_target_pairs={{0,1},{1,2},{2,3},{3,0},{4,5},{5,6},{6,7},{7,4},{8,9},{9,10},{10,1... | collective-permute-start | bytes 147464 | tf_op jit(solution)/shard_map/ppermute | solution.py:20
  17.2 5.5 %collective-permute-start.11 = (bf16[6,32,128]{2,1,0:T(8,128)(2,1)S(1)}, bf16[6,32,128]{2,1,0:T(8,128)(2,1)S(1)}, u32[]{:S(2)}, u32[]{:S(2)}) collective-permute-start(bf16[6,32,128]{2,1,0:T(8,128)(2,1)S(1)} %get-tuple-element.23), channel_id=1, source_target_pairs={{1,0},{2,1},{3,2},{0,3},{5,4},{6,5},{7,6},{4,7},{9,8},{10,9},{11,1... | collective-permute-start | bytes 147464 | tf_op jit(solution)/shard_map/ppermute | solution.py:23
  19.4 6.2 %collective-permute-start.6 = (bf16[8,32,256]{2,1,0:T(8,128)(2,1)S(1)}, bf16[8,32,256]{2,1,0:T(8,128)(2,1)S(1)}, u32[]{:S(2)}, u32[]{:S(2)}) collective-permute-start(bf16[8,32,256]{2,1,0:T(8,128)(2,1)S(1)} %get-tuple-element.20), channel_id=1, source_target_pairs={{0,1},{1,2},{2,3},{3,0},{4,5},{5,6},{6,7},{7,4},{8,9},{9,10},{10,1... | collective-permute-start | bytes 393224 | tf_op jit(solution)/shard_map/ppermute | solution.py:20
  19.9 5.8 %collective-permute-start.7 = (bf16[8,32,256]{2,1,0:T(8,128)(2,1)S(1)}, bf16[8,32,256]{2,1,0:T(8,128)(2,1)S(1)}, u32[]{:S(2)}, u32[]{:S(2)}) collective-permute-start(bf16[8,32,256]{2,1,0:T(8,128)(2,1)S(1)} %get-tuple-element.21), channel_id=1, source_target_pairs={{1,0},{2,1},{3,2},{0,3},{5,4},{6,5},{7,6},{4,7},{9,8},{10,9},{11,1... | collective-permute-start | bytes 393224 | tf_op jit(solution)/shard_map/ppermute | solution.py:23

commit v2 on v1

--- a/solution.py
+++ b/solution.py
@@ -12,16 +12,82 @@
 bf16 = jnp.bfloat16
 
 
-def halo(block, axis, dim, low_width, high_width):
-    count = lax.axis_size(axis)
-    forward = [(i, (i + 1) % count) for i in range(count)]
-    backward = [((i + 1) % count, i) for i in range(count)]
-    extent = block.shape[dim]
-    low = lax.ppermute(
-        lax.slice_in_dim(block, extent - low_width, None, axis=dim), axis, forward
-    )
-    high = lax.ppermute(lax.slice_in_dim(block, 0, high_width, axis=dim), axis, backward)
-    return jnp.concatenate([low, block, high], axis=dim)
+def span(step, extent, low, high):
+    if step > 0:
+        return (extent - low, low), (0, low)
+    if step < 0:
+        return (0, high), (low + extent, high)
+    return (0, extent), (low, extent)
+
+
+def fetch_body(plans, *refs):
+    count = len(plans)
+    ins, exts, (send, recv) = refs[:count], refs[count : 2 * count], refs[2 * count :]
+    steps = [(i, j) for i in (-1, 0, 1) for j in (-1, 0, 1) if (i, j) != (0, 0)]
+
+    def device(step):
+        place = {}
+        for axis, d in zip(("gx", "gy"), step):
+            size = lax.axis_size(axis)
+            place[axis] = lax.rem(lax.axis_index(axis) + size + d, size)
+        return place
+
+    barrier = pltpu.get_barrier_semaphore()
+    for step in steps:
+        pl.semaphore_signal(
+            barrier, inc=1, device_id=device(step), device_id_type=pl.DeviceIdType.MESH
+        )
+    pl.semaphore_wait(barrier, len(steps))
+    copies = []
+    for step in steps:
+        for src, dst, plan in zip(ins, exts, plans):
+            at_src, at_dst = [slice(None)] * len(src.shape), [slice(None)] * len(src.shape)
+            for d, (dim, unit, low, high) in zip(step, plan):
+                (s0, n0), (d0, n1) = span(d, src.shape[dim] // unit, low, high)
+                at_src[dim] = pl.ds(s0 * unit, n0 * unit)
+                at_dst[dim] = pl.ds(d0 * unit, n1 * unit)
+            k = len(copies)
+            copies.append(
+                pltpu.make_async_remote_copy(
+                    src_ref=src.at[tuple(at_src)],
+                    dst_ref=dst.at[tuple(at_dst)],
+                    send_sem=send.at[k],
+                    recv_sem=recv.at[k],
+                    device_id=device(step),
+                    device_id_type=pl.DeviceIdType.MESH,
+                )
+            )
+            copies[-1].start()
+    for src, dst, plan in zip(ins, exts, plans):
+        at = [slice(None)] * len(src.shape)
+        for dim, unit, low, high in plan:
+            at[dim] = slice(low * unit, low * unit + src.shape[dim])
+        dst[tuple(at)] = src[...]
+    for c in copies:
+        c.wait_recv()
+    for c in copies:
+        c.wait_send()
+
+
+def fetch(arrays, plans):
+    vmem = pl.BlockSpec(memory_space=pltpu.VMEM)
+    shapes = []
+    for v, plan in zip(arrays, plans):
+        shape = list(v.shape)
+        for dim, unit, low, high in plan:
+            shape[dim] += unit * (low + high)
+        shapes.append(jax.ShapeDtypeStruct(tuple(shape), v.dtype))
+    return pl.pallas_call(
+        functools.partial(fetch_body, plans),
+        out_shape=tuple(shapes),
+        in_specs=[vmem] * len(arrays),
+        out_specs=(vmem,) * len(arrays),
+        scratch_shapes=[pltpu.SemaphoreType.DMA((8 * len(arrays),))] * 2,
+        compiler_params=pltpu.CompilerParams(
+            collective_id=0, has_side_effects=True, vmem_limit_bytes=24 << 20
+        ),
+        name="fetch",
+    )(*arrays)
 
 
 def mm(lhs, rhs):
@@ -278,10 +344,15 @@
 
     skip = jnp.transpose(skip_field, (1, 0, 2, 3)).reshape(nx, ch, ny * nz)
     cot = jnp.transpose(cotangent, (1, 0, 2, 3)).reshape(nx, ch, ny * nz)
-    skip = halo(halo(skip, "gx", 0, 2, 2), "gy", 2, 2 * nz, 2 * nz)
-    cot = halo(halo(cot, "gx", 0, 1, 1), "gy", 2, nz, nz)
     coarse = jnp.transpose(coarse_field, (2, 1, 0, 3))
-    coarse = halo(halo(coarse, "gx", 1, 1, 2), "gy", 0, 1, 2)
+    skip, cot, coarse = fetch(
+        (skip, cot, coarse),
+        (
+            ((0, 1, 2, 2), (2, nz, 2, 2)),
+            ((0, 1, 1, 1), (2, nz, 1, 1)),
+            ((1, 1, 1, 2), (0, 1, 1, 2)),
+        ),
+    )
     coarse = coarse.reshape(hy + 3, (hx + 3) * ch, nz // 2)
 
     def up_weight(taps_a, taps_b):

time: 67.5 us -> 63.9 us (0.947)
  starting transfers between devices: 13.6 us -> 0 us
  Pallas kernels: 37.4 us -> 50.6 us
  waiting for transfers between devices: 4.49 us -> 0 us
  local copies, waits for them, and re-layouts: 10 us -> 12.1 us
    pallas_call x0 -> x1, Pallas kernels: none -> 17.9 us  [fetch(): pl.pallas_call(functools.partial(fetch_body, plans), out_shape=tuple(shap...]
    ppermute x12 -> x0, starting transfers between devices: 13.6 us -> none  [the longest x6 6.83 us: halo(): lax.ppermute(lax.slice_in_dim(block, 0, high_width, axis=dim), axis, back...]
    pallas_call x1, Pallas kernels: 27.3 us -> 22.6 us  [all_sum(): pl.pallas_call(functools.partial(reduce_body, ch), out_shape=(jax.ShapeDt...]
    ppermute x12 -> x0, waiting for transfers between devices: 4.49 us -> none  [the longest x6 4.48 us: halo(): lax.ppermute(lax.slice_in_dim(block, extent - low_width, None, axis=dim),...]
    unnamed x24 -> x19, local copies, waits for them, and re-layouts: 3.78 us -> 7.82 us
    slice x13 -> x0, local copies, waits for them, and re-layouts: 3.06 us -> none  [the longest x6 2.06 us: halo(): lax.slice_in_dim(block, 0, high_width, axis=dim)]
    transpose x2, local copies, waits for them, and re-layouts: 0.17 us -> 1.11 us  [local(): jnp.transpose(conv_kernel[:, :, ::-1, ::-1, :], (4, 1, 2, 3, 0))]
  transfers between devices with their start and end apart: 12 -> 0, of which waited for: 2 -> 0; matrix products, arithmetic and copies ran while one was open for 8% -> 0% of each run, Pallas kernels for 0% -> 0%
where the time goes in v2:
time: 63.9 us; the launch traced here: 63.6 us
  Pallas kernels  50.6 us (79%)
  local copies, waits for them, and re-layouts  12.1 us (19%)
  between operations  0.82 us (1%)
    pallas_call x1, Pallas kernels, all_sum(): pl.pallas_call(functools.partial(reduce_body, ch), out_shape=(jax.ShapeDt...  22.6 us
    pallas_call x1, Pallas kernels, fetch(): pl.pallas_call(functools.partial(fetch_body, plans), out_shape=tuple(shap...  17.9 us
    pallas_call x1, Pallas kernels, local(): pl.pallas_call(functools.partial(body, (ch, nx, ny, nz), scaling), out_sh...  10.2 us
    unnamed x19, local copies, waits for them, and re-layouts  7.82 us
    transpose x2, local copies, waits for them, and re-layouts, unpack(): return jnp.transpose(v.reshape(nx, ch, ny, nz), (1, 0, 2, 3))  1.5 us

profile of v2, /device:TPU:1, one launch (start us, length us, event | category | flops | bytes accessed | tf_op | source)
XLA Modules:
  0.0 63.6 jit_solution(9720647651582506488)
XLA Ops:
  0.6 0.6 %copy-done.4 = f32[32]{0:T(128)S(1)} copy-done((f32[32]{0:T(128)S(1)}, f32[32]{0:T(128)}, u32[]{:S(2)}) %copy-start.4) | copy-done | bytes 152
  1.4 0.6 copy-done.5
  2.0 0.8 %copy.45 = bf16[32,2,4,64]{3,0,1,2:T(8,128)(2,1)S(1)} copy(bf16[32,2,4,64]{3,2,1,0:T(4,128)(2,1)} %param.7) | data formatting | bytes 65536 | tf_op args[0]
  2.9 1.0 %reverse_bitcast_fusion = bf16[3,64,3,3,32]{1,4,0,3,2:T(8,128)(2,1)S(1)} fusion(bf16[32,64,3,3,3]{1,0,4,3,2:T(8,128)(2,1)} %param.12), kind=kLoop, calls=%fused_computation.2 | loop fusion | bytes 221184 | tf_op jit(solution)/shard_map/transpose | solution.py:364
  3.8 0.2 copy.32
  4.0 0.2 reshape.68
  4.2 0.1 copy.33.wa
  4.4 0.8 %copy-done.3 = bf16[32,32,3,3,3]{1,0,4,3,2:T(8,128)(2,1)S(1)} copy-done((bf16[32,32,3,3,3]{1,0,4,3,2:T(8,128)(2,1)S(1)}, bf16[32,32,3,3,3]{1,0,4,3,2:T(8,128)(2,1)}, u32[]{:S(2)}) %copy-start.3) | copy-done | bytes 55320
  5.3 0.1 reshape.66.woo
  5.5 0.1 reshape.64.weo
  5.7 0.6 copy-done.1
  6.5 0.9 %copy-done.2 = bf16[32,4,8,128]{3,2,1,0:T(8,128)(2,1)S(1)} copy-done((bf16[32,4,8,128]{3,2,1,0:T(8,128)(2,1)S(1)}, bf16[32,4,8,128]{3,2,1,0:T(8,128)(2,1)}, u32[]{:S(2)}) %copy-start.2) | copy-done | bytes 262168
  7.5 0.8 %copy-done = bf16[32,64,3,3,3]{1,0,4,3,2:T(8,128)(2,1)S(1)} copy-done((bf16[32,64,3,3,3]{1,0,4,3,2:T(8,128)(2,1)S(1)}, bf16[32,64,3,3,3]{1,0,4,3,2:T(8,128)(2,1)}, u32[]{:S(2)}) %copy-start) | copy-done | bytes 110616
  8.4 0.2 copy.31
  8.5 0.2 reshape.67.wf
  8.7 17.9 %fetch.1 = (bf16[8,32,1536]{2,1,0:T(8,128)(2,1)S(1)}, bf16[6,32,1280]{2,1,0:T(8,128)(2,1)S(1)}, bf16[7,5,32,64]{3,2,1,0:T(8,128)(2,1)S(1)}) custom-call(bf16[4,32,1024]{2,1,0:T(8,128)(2,1)S(1)} %copy.38.refs_0_, bf16[4,32,1024]{2,1,0:T(8,128)(2,1)S(1)} %copy.39.refs_1_, bf16[4,2,32,64]{3,2,1,0:T(8,128)(2,1)S(1)} %bitcast.81), custom_call_target="tpu_custom_call" | custom-call | tf_op jit(solution)/shard_map/fetch/pallas_call | solution.py:80
  26.6 10.2 %level.1 = (bf16[4,32,1024]{2,1,0:T(8,128)(2,1)S(1)}, bf16[4,32,1024]{2,1,0:T(8,128)(2,1)S(1)}, f32[896,128]{1,0:T(8,128)S(1)}) custom-call(bf16[7,160,64]{2,1,0:T(8,128)(2,1)S(1)} %bitcast.80, bf16[8,32,1536]{2,1,0:T(8,128)(2,1)S(1)} %get-tuple-element.17.skip, bf16[6,32,1280]{2,1,0:T(8,128)(2,1)S(1)} %get-tuple-element.18.cot, ...), custom_call_target="tpu_custom_call" | custom-call | tf_op jit(solution)/shard_map/level/pallas_call | solution.py:369
  36.9 0.8 %copy_bitcast_fusion.1 = bf16[32,4,8,128]{3,2,1,0:T(8,128)(2,1)} fusion(bf16[4,32,8,128]{3,2,1,0:T(8,128)(2,1)S(1)} %bitcast.87), kind=kLoop, calls=%fused_computation.1 | loop fusion | bytes 524288 | tf_op jit(solution)/shard_map/transpose | solution.py:396
  37.7 0.8 %copy_bitcast_fusion = bf16[32,4,8,128]{3,2,1,0:T(8,128)(2,1)} fusion(bf16[4,32,8,128]{3,2,1,0:T(8,128)(2,1)S(1)} %bitcast.88), kind=kLoop, calls=%fused_computation | loop fusion | bytes 524288 | tf_op jit(solution)/shard_map/transpose | solution.py:396
  38.4 22.6 %total.1 = (f32[27,32,64]{2,1,0:T(8,128)S(1)}, f32[1,32]{1,0:T(1,128)S(1)}, f32[27,32,32]{2,1,0:T(8,128)S(1)}, f32[1,32]{1,0:T(1,128)S(1)}) custom-call(f32[4,4,56,128]{3,2,1,0:T(8,128)S(1)} %bitcast.77), custom_call_target="tpu_custom_call" | custom-call | tf_op jit(solution)/shard_map/total/pallas_call | solution.py:314
  61.0 0.8 %copy.50 = f32[32,64,3,3,3]{1,0,4,3,2:T(8,128)} copy(f32[32,64,3,3,3]{1,0,4,3,2:T(8,128)S(1)} %bitcast.79) | data formatting | bytes 442368
  61.8 0.5 copy.51
  62.3 0.8 %copy.52 = f32[32,32,3,3,3]{1,0,4,3,2:T(8,128)} copy(f32[32,32,3,3,3]{1,0,4,3,2:T(8,128)S(1)} %bitcast.78) | data formatting | bytes 221184
  63.0 0.5 copy.53
  (21 shorter events, 0.9 us)
Async XLA Ops:
  0.6 0.7 %copy-start.4 = (f32[32]{0:T(128)S(1)}, f32[32]{0:T(128)}, u32[]{:S(2)}) copy-start(f32[32]{0:T(128)} %param.11) | copy-start | bytes 388
  1.3 0.7 %copy-start.5 = (f32[32]{0:T(128)S(1)}, f32[32]{0:T(128)}, u32[]{:S(2)}) copy-start(f32[32]{0:T(128)} %param.13) | copy-start | bytes 388
  4.2 0.9 %copy-start.3 = (bf16[32,32,3,3,3]{1,0,4,3,2:T(8,128)(2,1)S(1)}, bf16[32,32,3,3,3]{1,0,4,3,2:T(8,128)(2,1)}, u32[]{:S(2)}) copy-start(bf16[32,32,3,3,3]{1,0,4,3,2:T(8,128)(2,1)} %param.10) | copy-start | bytes 165892
  5.4 1.0 %copy-start.1 = (bf16[32,4,8,128]{3,2,1,0:T(8,128)(2,1)S(1)}, bf16[32,4,8,128]{3,2,1,0:T(8,128)(2,1)}, u32[]{:S(2)}) copy-start(bf16[32,4,8,128]{3,2,1,0:T(8,128)(2,1)} %param.8) | copy-start | bytes 786436
  6.4 1.0 %copy-start.2 = (bf16[32,4,8,128]{3,2,1,0:T(8,128)(2,1)S(1)}, bf16[32,4,8,128]{3,2,1,0:T(8,128)(2,1)}, u32[]{:S(2)}) copy-start(bf16[32,4,8,128]{3,2,1,0:T(8,128)(2,1)} %param.9) | copy-start | bytes 786436
  7.4 0.9 %copy-start = (bf16[32,64,3,3,3]{1,0,4,3,2:T(8,128)(2,1)S(1)}, bf16[32,64,3,3,3]{1,0,4,3,2:T(8,128)(2,1)}, u32[]{:S(2)}) copy-start(bf16[32,64,3,3,3]{1,0,4,3,2:T(8,128)(2,1)} %param.12) | copy-start | bytes 331780
